TPU v7x, 32 devices: a whole 2x2x4 slice. The times are simulated.
32 devices in a mesh: pipe: 4 (over z), dp: 4 (over x, core), expert: 2 (over y).
Axes of the slice: x: 2, y: 2, z: 4, core: 2. Of those that a mesh axis runs over, the one named last changes fastest.
Arguments:
- block_input: bfloat16 [4, 1024, 3072], P('pipe', ('dp', 'expert')), may hold values from -6 to 6
- output_grad: bfloat16 [4, 1024, 3072], P('pipe', ('dp', 'expert')), may hold values from -6 to 6
- expert_ids: int32 [4, 1024, 6], P('pipe', ('dp', 'expert')), may hold values from 0 to 159, all different within a row
- gate_weights: float32 [4, 1024, 6], P('pipe', ('dp', 'expert')), may hold values from 0.25 to 2
- gate_proj: bfloat16 [4, 2, 3072, 1024], P('pipe', 'expert', None, 'dp'), may hold values from -0.109375 to 0.109375
- up_proj: bfloat16 [4, 2, 3072, 1024], P('pipe', 'expert', None, 'dp'), may hold values from -0.109375 to 0.109375
- down_proj: bfloat16 [4, 2, 1024, 3072], P('pipe', 'expert', 'dp'), may hold values from -0.1875 to 0.1875
Outputs:
- received_grad: bfloat16 [4, 1024, 3072], P('pipe', ('dp', 'expert'))
- gate_weight_grad: float32 [4, 1024, 6], P('pipe', ('dp', 'expert'))
- gate_proj_grad: bfloat16 [4, 2, 3072, 1024], P('pipe', 'expert', None, 'dp')
- up_proj_grad: bfloat16 [4, 2, 3072, 1024], P('pipe', 'expert', None, 'dp')
- down_proj_grad: bfloat16 [4, 2, 1024, 3072], P('pipe', 'expert', 'dp')
Inputs may be any that keep to these rules, and one draw needn't show every extreme that they name: `expert_ids`: each token names 6 different experts.
All inputs are finite; a program needn't handle non-finite values.
Results may differ from a plain program's by a relative error of at most 0.006.
Values may be sent and summed in bfloat16 or wider, within the bound.
No kernel may reach another device: no remote copies, remote signals or barrier semaphores. Data moves between devices by JAX's collectives and lax.ppermute only.
A program may use at most 128 MiB of HBM per device.

v0:
```python
import jax
import jax.numpy as jnp
from jax import lax
from jax.sharding import PartitionSpec as P


def shifted(value, axis, steps):
    count = lax.axis_size(axis)
    pairs = [(source, (source + steps) % count) for source in range(count)]
    return lax.ppermute(value, axis, pairs)


def slot_tables(chosen_ids, experts, capacity):
    tok_count, chosen = chosen_ids.shape
    flat_ids = chosen_ids.reshape(-1)
    columns = jnp.arange(experts, dtype=jnp.int32)
    onehot = (flat_ids[:, None] == columns[None, :]).astype(jnp.int32)
    earlier = jnp.cumsum(onehot, axis=0) - onehot
    slot_rank = jnp.sum(earlier * onehot, axis=1)
    kept_pair = (flat_ids < experts) & (slot_rank < capacity)
    slot_index = jnp.where(kept_pair, flat_ids * capacity + slot_rank, experts * capacity)
    slot_rows = jnp.arange(experts * capacity, dtype=jnp.int32)
    placed = slot_index[None, :] == slot_rows[:, None]
    pair_index = jnp.arange(tok_count * chosen, dtype=jnp.int32)
    source_pair = jnp.sum(jnp.where(placed, pair_index[None, :], 0), axis=1)
    filled = jnp.any(placed, axis=1)
    return (slot_index, source_pair, filled)


def shards(block_input, output_grad, expert_ids, gate_weights, gate_proj, up_proj, down_proj):
    acts_local = block_input[0]
    grad_local = output_grad[0]
    chosen_ids = expert_ids[0]
    route_weight = gate_weights[0]
    tok_count, chosen = chosen_ids.shape
    width = acts_local.shape[1]
    local_count = gate_proj.shape[1]
    dp_count = lax.axis_size("dp")
    expert_count = lax.axis_size("expert")
    experts = local_count * expert_count
    capacity = tok_count // 16
    slot_index, source_pair, filled = slot_tables(chosen_ids, experts, capacity)
    source_token = source_pair // chosen
    slot_weight = route_weight.reshape(-1)[source_pair]
    send_acts = jnp.where(filled[:, None], acts_local[source_token], jnp.zeros((), jnp.bfloat16))
    scaled = slot_weight[:, None] * grad_local[source_token].astype(jnp.float32)
    send_grad = jnp.where(filled[:, None], scaled, 0.0).astype(jnp.bfloat16)
    send_acts = send_acts.reshape(experts, capacity, width)
    send_grad = send_grad.reshape(experts, capacity, width)
    acts_copies = jnp.broadcast_to(send_acts[None], (dp_count,) + send_acts.shape).reshape(
        dp_count * experts, capacity, width
    )
    grad_copies = jnp.broadcast_to(send_grad[None], (dp_count,) + send_grad.shape).reshape(
        dp_count * experts, capacity, width
    )
    recv_acts, recv_grad = (
        lax.all_to_all(acts_copies, ("dp", "expert"), split_axis=0, concat_axis=1, tiled=True),
        lax.all_to_all(grad_copies, ("dp", "expert"), split_axis=0, concat_axis=1, tiled=True),
    )
    gate_local = gate_proj[0]
    upper_local = up_proj[0]
    lower_local = down_proj[0]
    gate_pre = jnp.einsum("erd,edh->erh", recv_acts, gate_local, preferred_element_type=jnp.float32)
    up_value = jnp.einsum(
        "erd,edh->erh", recv_acts, upper_local, preferred_element_type=jnp.float32
    )
    grad_hidden = jnp.einsum(
        "erd,ehd->erh", recv_grad, lower_local, preferred_element_type=jnp.float32
    )
    sigma_gate = jax.nn.sigmoid(gate_pre)
    swish = gate_pre * sigma_gate
    hidden = swish * up_value
    scores = jnp.sum(hidden * grad_hidden, axis=2)
    lower_grad = jnp.einsum(
        "erh,erd->ehd", hidden.astype(jnp.bfloat16), recv_grad, preferred_element_type=jnp.float32
    ).astype(jnp.bfloat16)
    delta_gate = (
        grad_hidden * up_value * sigma_gate * (1.0 + gate_pre * (1.0 - sigma_gate))
    ).astype(jnp.bfloat16)
    delta_up = (grad_hidden * swish).astype(jnp.bfloat16)
    gate_grad = jnp.einsum(
        "erd,erh->edh", recv_acts, delta_gate, preferred_element_type=jnp.float32
    ).astype(jnp.bfloat16)
    upper_grad = jnp.einsum(
        "erd,erh->edh", recv_acts, delta_up, preferred_element_type=jnp.float32
    ).astype(jnp.bfloat16)
    partial_value = jnp.einsum(
        "erh,edh->erd", delta_gate, gate_local, preferred_element_type=jnp.float32
    ) + jnp.einsum("erh,edh->erd", delta_up, upper_local, preferred_element_type=jnp.float32)
    back_rows, back_scores = (
        lax.all_to_all(partial_value, ("dp", "expert"), split_axis=1, concat_axis=0, tiled=True),
        lax.all_to_all(scores, ("dp", "expert"), split_axis=1, concat_axis=0, tiled=True),
    )
    slot_grad = jnp.sum(back_rows.reshape(dp_count, experts * capacity, width), axis=0).astype(
        jnp.bfloat16
    )
    slot_scores = jnp.sum(back_scores.reshape(dp_count, experts * capacity), axis=0)
    token_rows = jnp.arange(tok_count, dtype=jnp.int32)
    token_map = ((source_token[:, None] == token_rows[None, :]) & filled[:, None]).astype(
        jnp.bfloat16
    )
    input_grad = jnp.einsum(
        "st,sd->td", token_map, slot_grad, preferred_element_type=jnp.float32
    ).astype(jnp.bfloat16)
    padded_scores = jnp.concatenate([slot_scores, jnp.zeros((1,), jnp.float32)])
    weight_grad = (padded_scores[slot_index] / route_weight.reshape(-1)).reshape(tok_count, chosen)
    received = shifted(input_grad, "pipe", -1)
    return (received[None], weight_grad[None], gate_grad[None], upper_grad[None], lower_grad[None])


def solution(mesh):
    in_specs = (
        P("pipe", ("dp", "expert"), None),
        P("pipe", ("dp", "expert"), None),
        P("pipe", ("dp", "expert"), None),
        P("pipe", ("dp", "expert"), None),
        P("pipe", "expert", None, "dp"),
        P("pipe", "expert", None, "dp"),
        P("pipe", "expert", "dp", None),
    )
    out_specs = (
        P("pipe", ("dp", "expert"), None),
        P("pipe", ("dp", "expert"), None),
        P("pipe", "expert", None, "dp"),
        P("pipe", "expert", None, "dp"),
        P("pipe", "expert", "dp", None),
    )
    return jax.shard_map(shards, mesh=mesh, in_specs=in_specs, out_specs=out_specs, check_vma=False)
```

profile of v0, /device:TPU:0, one launch (start us, length us, event | category | flops | bytes accessed | tf_op | source)
XLA Modules:
  0.0 79.5 jit_solution(6049653979190262560)
XLA Ops:
  0.7 0.9 %copy.28 = s32[1,128,6]{2,1,0:T(8,128)S(1)} copy(s32[1,128,6]{1,0,2:T(1,128)} %param.9) | data formatting | bytes 6144 | tf_op args[2]
  3.3 1.9 %gather_fusion.2 = bf16[16,3072]{1,0:T(8,128)(2,1)S(1)} fusion(bf16[128,3072]{1,0:T(8,128)(2,1)} %bitcast.109, s32[1024]{0:T(1024)S(1)} %get-tuple-element.53), kind=kCustom, calls=%fused_computation.2 | custom fusion | bytes 196672 | tf_op jit(solution)/shard_map/gather | solution.py:45
  6.1 5.2 %all-to-all-start.1 = ((bf16[8,8,3072]{2,1,0:T(8,128)(2,1)}), bf16[8,8,3072]{2,1,0:T(8,128)(2,1)S(1)}, u32[]{:S(2)}, u32[]{:S(2)}) async-start(bf16[8,8,3072]{2,1,0:T(8,128)(2,1)} %bitcast.11), calls=%async_computation.1 | async-start | bytes 786432 | tf_op jit(solution)/shard_map/all_to_all | solution.py:57
  14.0 4.7 %all-to-all-done.1 = bf16[8,8,3072]{2,1,0:T(8,128)(2,1)S(1)} async-done(((bf16[8,8,3072]{2,1,0:T(8,128)(2,1)}), bf16[8,8,3072]{2,1,0:T(8,128)(2,1)S(1)}, u32[]{:S(2)}, u32[]{:S(2)}) %all-to-all-start.1) | async-done | bytes 393248 | tf_op jit(solution)/shard_map/all_to_all | solution.py:57
  18.7 1.7 %broadcast_in_dim.84 = bf16[4,2,8,3072]{3,2,1,0:T(8,128)(2,1)} broadcast(bf16[2,8,3072]{2,1,0:T(8,128)(2,1)} %fusion.20), dimensions={1,2,3} | broadcast | bytes 491520 | tf_op jit(solution)/shard_map/broadcast_in_dim | solution.py:53
  20.4 4.1 %all-to-all-start = ((bf16[8,8,3072]{2,1,0:T(8,128)(2,1)}), bf16[8,8,3072]{2,1,0:T(8,128)(2,1)}, u32[]{:S(2)}, u32[]{:S(2)}) async-start(bf16[8,8,3072]{2,1,0:T(8,128)(2,1)} %bitcast.108), calls=%async_computation | async-start | bytes 786432 | tf_op jit(solution)/shard_map/all_to_all | solution.py:58
  24.5 1.0 %fusion.6 = f32[64,256]{1,0:T(8,128)} fusion(bf16[1,1,3072,256]{3,2,1,0:T(8,128)(2,1)S(1)} %copy-done, bf16[8,8,3072]{2,1,0:T(8,128)(2,1)S(1)} %all-to-all-done.1), kind=kOutput, calls=%fused_computation.14 | convolution fusion | flops 100663296 | bytes 2031616 | tf_op jit(solution)/shard_map/erd,edh->erh/dot_general | solution.py:63
  25.5 1.0 %fusion.9 = f32[64,256]{1,0:T(8,128)} fusion(bf16[1,1,3072,256]{3,2,1,0:T(8,128)(2,1)S(1)} %copy-done.1, bf16[8,8,3072]{2,1,0:T(8,128)(2,1)S(1)} %all-to-all-done.1), kind=kOutput, calls=%fused_computation.17 | convolution fusion | flops 100663296 | bytes 2031616 | tf_op jit(solution)/shard_map/erd,edh->erh/dot_general | solution.py:64
  26.5 5.4 %all-to-all-done = bf16[8,8,3072]{2,1,0:T(8,128)(2,1)} async-done(((bf16[8,8,3072]{2,1,0:T(8,128)(2,1)}), bf16[8,8,3072]{2,1,0:T(8,128)(2,1)}, u32[]{:S(2)}, u32[]{:S(2)}) %all-to-all-start) | async-done | bytes 393248 | tf_op jit(solution)/shard_map/all_to_all | solution.py:58
  31.9 2.7 %multiply_reduce_fusion = (f32[64]{0:T(128)}, bf16[64,256]{1,0:T(8,128)(2,1)S(1)}, bf16[64,256]{1,0:T(8,128)(2,1)S(1)}) fusion(f32[64,256]{1,0:T(8,128)} %fusion.9, f32[64,256]{1,0:T(8,128)} %fusion.6, bf16[1,1,256,3072]{3,2,1,0:T(8,128)(2,1)} %param.13, bf16[8,8,3072]{2,1,0:T(8,128)(2,1)} %all-to-all-done), kind=kOutput, calls=%fused_computation.32 | convolution fusion | flops 100925376 | bytes 2162944 | tf_op jit(solution)/shard_map/erd,ehd->erh/dot_general | solution.py:67
  35.9 1.7 %copy.31 = f32[1,64,3072]{2,0,1:T(1,128)} copy(f32[1,64,3072]{2,1,0:T(8,128)S(1)} %fusion.3) | data formatting | bytes 1572864 | tf_op jit(solution)/shard_map/add | solution.py:87
  37.6 3.7 %all-to-all-start.2 = ((f32[1,64,3072]{2,0,1:T(1,128)}), f32[1,64,3072]{2,0,1:T(1,128)S(1)}, u32[]{:S(2)}, u32[]{:S(2)}) async-start(f32[1,64,3072]{2,0,1:T(1,128)} %copy.31), calls=%async_computation.2 | async-start | bytes 1572864 | tf_op jit(solution)/shard_map/all_to_all | solution.py:91
  42.8 1.7 %fusion.1 = bf16[1,1,3072,256]{3,2,1,0:T(8,128)(2,1)} fusion(bf16[64,256]{1,0:T(8,128)(2,1)S(1)} %copy-done.8, bf16[8,8,3072]{2,1,0:T(8,128)(2,1)S(1)} %all-to-all-done.1), kind=kOutput, calls=%fused_computation.7 | convolution fusion | flops 101449728 | bytes 1998848 | tf_op jit(solution)/shard_map/erd,erh->edh/dot_general | solution.py:84
  44.6 2.7 %fusion.2 = bf16[1,1,256,3072]{3,2,1,0:T(8,128)(2,1)} fusion(bf16[8,8,3072]{2,1,0:T(8,128)(2,1)} %all-to-all-done, f32[64,256]{1,0:T(8,128)S(1)} %copy-done.4, f32[64,256]{1,0:T(8,128)S(1)} %copy-done.3), kind=kOutput, calls=%fused_computation.8 | convolution fusion | flops 101548032 | bytes 2097152 | tf_op jit(solution)/shard_map/erh,erd->ehd/dot_general | solution.py:74
  47.3 5.6 %all-to-all-done.2 = f32[1,64,3072]{2,0,1:T(1,128)S(1)} async-done(((f32[1,64,3072]{2,0,1:T(1,128)}), f32[1,64,3072]{2,0,1:T(1,128)S(1)}, u32[]{:S(2)}, u32[]{:S(2)}) %all-to-all-start.2) | async-done | bytes 786464 | tf_op jit(solution)/shard_map/all_to_all | solution.py:91
  52.9 3.3 %all-to-all-start.3 = ((f32[1,8,8]{2,0,1:T(1,128)}), f32[1,8,8]{2,0,1:T(1,128)S(1)}, u32[]{:S(2)}, u32[]{:S(2)}) async-start(f32[1,8,8]{2,0,1:T(1,128)} %bitcast.17), calls=%async_computation.3 | async-start | bytes 8192 | tf_op jit(solution)/shard_map/all_to_all | solution.py:92
  56.4 1.2 %convolution_convert_fusion.3 = bf16[128,3072]{1,0:T(8,128)(2,1)S(1)} fusion(bf16[16,3072]{1,0:T(8,128)(2,1)S(1)} %reduce_sum.52, s32[16]{0:T(128)} %and_select_fusion.2, pred[16]{0:T(512)(128)(4,1)} %copy-done.11), kind=kOutput, calls=%fused_computation.9 | convolution fusion | flops 12980224 | bytes 884816 | tf_op jit(solution)/shard_map/st,sd->td/dot_general | solution.py:102
  57.6 3.7 %collective-permute-start = (bf16[128,3072]{1,0:T(8,128)(2,1)S(1)}, bf16[128,3072]{1,0:T(8,128)(2,1)S(1)}, u32[]{:S(2)}, u32[]{:S(2)}) collective-permute-start(bf16[128,3072]{1,0:T(8,128)(2,1)S(1)} %convolution_convert_fusion.3), channel_id=1, source_target_pairs={{0,24},{8,0},{16,8},{24,16},{1,25},{9,1},{17,9},{25,17},{2,26},{10... | collective-permute-start | bytes 2359304 | tf_op jit(solution)/shard_map/ppermute | solution.py:10
  61.2 2.5 %fusion = bf16[1,1,3072,256]{3,2,1,0:T(8,128)(2,1)} fusion(bf16[64,256]{1,0:T(8,128)(2,1)} %copy-done.6, bf16[8,8,3072]{2,1,0:T(8,128)(2,1)S(1)} %all-to-all-done.1), kind=kOutput, calls=%fused_computation.6 | convolution fusion | flops 101449728 | bytes 1998848 | tf_op jit(solution)/shard_map/erd,erh->edh/dot_general | solution.py:81
  65.7 4.4 %fusion.34 = (f32[768]{0:T(1024)S(1)}, s32[768,1]{0,1:T(1,128)S(1)}) fusion(f32[]{:T(128)} %bitcast.27, f32[]{:T(128)} %bitcast.28, f32[]{:T(128)} %bitcast.29, f32[]{:T(128)} %bitcast.30, f32[]{:T(128)} %bitcast.31, f32[]{:T(128)} %bitcast.33, f32[]{:T(128)} %bitcast.32, s32[768,1]{0,1:T(1,128)S(1)} %mul.82, pred[768,1]{0,1:T(4,128)(4,1)S(1)} %lt.81, ...), kind=kLoop, calls=%fused_computation.76 | loop fusion | flops 14592 | bytes 13084 | tf_op jit(solution)/shard_map/gather | solution.py:106
  70.2 5.6 %select_select_fusion = f32[768]{0:T(1024)S(1)} fusion(pred[768]{0:T(1024)(128)(4,1)S(1)} %get-tuple-element.29, pred[768]{0:T(1024)(128)(4,1)S(1)} %get-tuple-element.28, pred[768]{0:T(1024)(128)(4,1)S(1)} %get-tuple-element.27, pred[768]{0:T(1024)(128)(4,1)S(1)} %get-tuple-element.26, pred[768]{0:T(1024)(128)(4,1)S(1)} %get-tuple-element.25, ...), kind=kLoop, calls=%fused_computation.72 | loop fusion | flops 7680 | bytes 13860 | tf_op jit(solution)/shard_map/gather | solution.py:106
  76.0 0.9 %div.29 = f32[1,128,6]{2,1,0:T(8,128)S(1)} divide(f32[1,128,6]{2,1,0:T(8,128)S(1)} %gather.21, f32[1,128,6]{2,1,0:T(8,128)} %copy-done.5) | non-fusion elementwise | flops 768 | bytes 9216 | tf_op jit(solution)/shard_map/div | solution.py:106
  77.5 1.0 %collective-permute-done = bf16[128,3072]{1,0:T(8,128)(2,1)S(1)} collective-permute-done((bf16[128,3072]{1,0:T(8,128)(2,1)S(1)}, bf16[128,3072]{1,0:T(8,128)(2,1)S(1)}, u32[]{:S(2)}, u32[]{:S(2)}) %collective-permute-start) | collective-permute-done | bytes 786464 | tf_op jit(solution)/shard_map/ppermute | solution.py:10
  78.6 0.9 %copy.41 = bf16[1,128,3072]{2,1,0:T(8,128)(2,1)} copy(bf16[1,128,3072]{2,1,0:T(8,128)(2,1)S(1)} %bitcast.111) | data formatting | bytes 1572864
  (73 shorter events, 11.0 us)
Async XLA Ops:
  0.6 23.9 %copy-start = (bf16[1,1,3072,256]{3,2,1,0:T(8,128)(2,1)S(1)}, bf16[1,1,3072,256]{3,2,1,0:T(8,128)(2,1)}, u32[]{:S(2)}) copy-start(bf16[1,1,3072,256]{3,2,1,0:T(8,128)(2,1)} %param.11) | copy-start | bytes 4718596
  0.6 10.7 %copy-start.9 = (s32[1,128,6]{1,0,2:T(1,128)S(1)}, s32[1,128,6]{1,0,2:T(1,128)}, u32[]{:S(2)}) copy-start(s32[1,128,6]{1,0,2:T(1,128)} %param.9) | copy-start | bytes 9220
  0.7 11.0 %copy-start.10 = (f32[1,128,6]{1,0,2:T(1,128)S(1)}, f32[1,128,6]{1,0,2:T(1,128)}, u32[]{:S(2)}) copy-start(f32[1,128,6]{1,0,2:T(1,128)} %param.10) | copy-start | bytes 9220
  2.8 9.8 %copy-start.2 = (bf16[1,128,3072]{2,1,0:T(8,128)(2,1)S(1)}, bf16[1,128,3072]{2,1,0:T(8,128)(2,1)}, u32[]{:S(2)}) copy-start(bf16[1,128,3072]{2,1,0:T(8,128)(2,1)} %param.8) | copy-start | bytes 2359300
  3.1 9.5 %copy-start.11 = (pred[16]{0:T(512)(128)(4,1)}, pred[16]{0:T(512)(128)(4,1)S(1)}, u32[]{:S(2)}) copy-start(pred[16]{0:T(512)(128)(4,1)S(1)} %fusion.23) | copy-start | bytes 52
  3.2 9.4 %copy-start.13 = (s32[16]{0:T(128)}, s32[16]{0:T(128)S(1)}, u32[]{:S(2)}) copy-start(s32[16]{0:T(128)S(1)} %select_reduce_fusion) | copy-start | bytes 196
  6.1 12.6 %all-to-all-start.1 = ((bf16[8,8,3072]{2,1,0:T(8,128)(2,1)}), bf16[8,8,3072]{2,1,0:T(8,128)(2,1)S(1)}, u32[]{:S(2)}, u32[]{:S(2)}) async-start(bf16[8,8,3072]{2,1,0:T(8,128)(2,1)} %bitcast.11), calls=%async_computation.1 | async-start | bytes 786432 | tf_op jit(solution)/shard_map/all_to_all | solution.py:57
  11.8 1.5 %copy-start.5 = (f32[1,128,6]{2,1,0:T(8,128)}, f32[1,128,6]{2,1,0:T(8,128)S(1)}, u32[]{:S(2)}) copy-start(f32[1,128,6]{2,1,0:T(8,128)S(1)} %copy.30) | copy-start | bytes 9220
  14.0 11.5 %copy-start.1 = (bf16[1,1,3072,256]{3,2,1,0:T(8,128)(2,1)S(1)}, bf16[1,1,3072,256]{3,2,1,0:T(8,128)(2,1)}, u32[]{:S(2)}) copy-start(bf16[1,1,3072,256]{3,2,1,0:T(8,128)(2,1)} %param.12) | copy-start | bytes 4718596
  20.4 11.5 %all-to-all-start = ((bf16[8,8,3072]{2,1,0:T(8,128)(2,1)}), bf16[8,8,3072]{2,1,0:T(8,128)(2,1)}, u32[]{:S(2)}, u32[]{:S(2)}) async-start(bf16[8,8,3072]{2,1,0:T(8,128)(2,1)} %bitcast.108), calls=%async_computation | async-start | bytes 786432 | tf_op jit(solution)/shard_map/all_to_all | solution.py:58
  34.6 0.6 copy-start.6
  34.6 0.6 copy-start.7
  35.9 5.7 %copy-start.14 = (s32[16]{0:T(128)S(1)}, s32[16]{0:T(128)}, u32[]{:S(2)}) copy-start(s32[16]{0:T(128)} %copy-done.13) | copy-start | bytes 196
  35.9 6.3 %copy-start.12 = (f32[64]{0:T(128)S(1)}, f32[64]{0:T(128)}, u32[]{:S(2)}) copy-start(f32[64]{0:T(128)} %get-tuple-element.32) | copy-start | bytes 772
  35.9 7.0 %copy-start.8 = (bf16[64,256]{1,0:T(8,128)(2,1)S(1)}, bf16[64,256]{1,0:T(8,128)(2,1)}, u32[]{:S(2)}) copy-start(bf16[64,256]{1,0:T(8,128)(2,1)} %copy-done.7) | copy-start | bytes 98308
  37.6 7.0 %copy-start.3 = (f32[64,256]{1,0:T(8,128)S(1)}, f32[64,256]{1,0:T(8,128)}, u32[]{:S(2)}) copy-start(f32[64,256]{1,0:T(8,128)} %fusion.6) | copy-start | bytes 196612
  37.6 7.0 %copy-start.4 = (f32[64,256]{1,0:T(8,128)S(1)}, f32[64,256]{1,0:T(8,128)}, u32[]{:S(2)}) copy-start(f32[64,256]{1,0:T(8,128)} %fusion.9) | copy-start | bytes 196612
  37.6 15.3 %all-to-all-start.2 = ((f32[1,64,3072]{2,0,1:T(1,128)}), f32[1,64,3072]{2,0,1:T(1,128)S(1)}, u32[]{:S(2)}, u32[]{:S(2)}) async-start(f32[1,64,3072]{2,0,1:T(1,128)} %copy.31), calls=%async_computation.2 | async-start | bytes 1572864 | tf_op jit(solution)/shard_map/all_to_all | solution.py:91
  52.9 10.8 %all-to-all-start.3 = ((f32[1,8,8]{2,0,1:T(1,128)}), f32[1,8,8]{2,0,1:T(1,128)S(1)}, u32[]{:S(2)}, u32[]{:S(2)}) async-start(f32[1,8,8]{2,0,1:T(1,128)} %bitcast.17), calls=%async_computation.3 | async-start | bytes 8192 | tf_op jit(solution)/shard_map/all_to_all | solution.py:92
  57.6 21.0 %collective-permute-start = (bf16[128,3072]{1,0:T(8,128)(2,1)S(1)}, bf16[128,3072]{1,0:T(8,128)(2,1)S(1)}, u32[]{:S(2)}, u32[]{:S(2)}) collective-permute-start(bf16[128,3072]{1,0:T(8,128)(2,1)S(1)} %convolution_convert_fusion.3), channel_id=1, source_target_pairs={{0,24},{8,0},{16,8},{24,16},{1,25},{9,1},{17,9},{25,17},{2,26},{10... | collective-permute-start | bytes 2359304 | tf_op jit(solution)/shard_map/ppermute | solution.py:10
where the time goes:
time: 80.3 us; the launch traced here: 79.5 us
  starting transfers between devices  19.9 us (25%)
  waiting for transfers between devices  16.7 us (21%)
  other arithmetic  14.3 us (18%)
  matrix products  14.1 us (18%)
  local copies, waits for them, and re-layouts  13.5 us (17%)
  between operations  0.92 us (1%)
    gather x3, other arithmetic, shards(): padded_scores[slot_index] / route_weight.reshape(-1)  10.2 us
    all_to_all x1, waiting for transfers between devices, shards(): lax.all_to_all(partial_value, ('dp', 'expert'), split_axis=1, concat_axis...  5.58 us
    all_to_all x1, waiting for transfers between devices, shards(): lax.all_to_all(grad_copies, ('dp', 'expert'), split_axis=0, concat_axis=1...  5.38 us
    all_to_all x1, starting transfers between devices, shards(): lax.all_to_all(acts_copies, ('dp', 'expert'), split_axis=0, concat_axis=1...  5.2 us
    all_to_all x1, waiting for transfers between devices, shards(): lax.all_to_all(acts_copies, ('dp', 'expert'), split_axis=0, concat_axis=1...  4.73 us
    all_to_all x1, starting transfers between devices, shards(): lax.all_to_all(grad_copies, ('dp', 'expert'), split_axis=0, concat_axis=1...  4.1 us
    all_to_all x1, starting transfers between devices, shards(): lax.all_to_all(partial_value, ('dp', 'expert'), split_axis=1, concat_axis...  3.68 us
    ppermute x1, starting transfers between devices, shifted(): return lax.ppermute(value, axis, pairs)  3.66 us
  transfers between devices with their start and end apart: 5, of which 4 were waited for; matrix products, arithmetic and copies ran while one was open for 35% of the time, Pallas kernels for 0%

commit v1 on v0

--- a/solution.py
+++ b/solution.py
@@ -54,7 +54,15 @@
         dp_count * experts, capacity, width
     )
     recv_acts, recv_grad = (
-        lax.all_to_all(acts_copies, ("dp", "expert"), split_axis=0, concat_axis=1, tiled=True),
+        jnp.concatenate(
+            lax.all_to_all(
+                jnp.stack(jnp.split(acts_copies, lax.axis_size(("dp", "expert")), axis=0)),
+                ("dp", "expert"),
+                0,
+                0,
+            ),
+            axis=1,
+        ),
         lax.all_to_all(grad_copies, ("dp", "expert"), split_axis=0, concat_axis=1, tiled=True),
     )
     gate_local = gate_proj[0]

time: 80.3 us -> 85 us (1.059)
  local copies, waits for them, and re-layouts: 13.5 us -> 18.2 us
    unnamed x35 -> x42, local copies, waits for them, and re-layouts: 2.79 us -> 7.57 us
  transfers between devices with their start and end apart: 5 -> 5, of which waited for: 4 -> 4; matrix products, arithmetic and copies ran while one was open for 35% -> 33% of each run, Pallas kernels for 0% -> 0%
where the time goes in v1:
time: 85 us; the launch traced here: 84.2 us
  starting transfers between devices  19.9 us (23%)
  local copies, waits for them, and re-layouts  18.2 us (21%)
  waiting for transfers between devices  16.7 us (20%)
  other arithmetic  14.3 us (17%)
  matrix products  14.1 us (17%)
  between operations  0.91 us (1%)
    gather x3, other arithmetic, shards(): padded_scores[slot_index] / route_weight.reshape(-1)  10.2 us
    unnamed x42, local copies, waits for them, and re-layouts  7.57 us
    all_to_all x1, waiting for transfers between devices, shards(): lax.all_to_all(partial_value, ('dp', 'expert'), split_axis=1, concat_axis...  5.58 us
    all_to_all x1, waiting for transfers between devices, shards(): lax.all_to_all(grad_copies, ('dp', 'expert'), split_axis=0, concat_axis=1...  5.38 us
    all_to_all x1, starting transfers between devices, shards(): lax.all_to_all(jnp.stack(jnp.split(acts_copies, lax.axis_size(('dp', 'exp...  5.2 us
    all_to_all x1, waiting for transfers between devices, shards(): lax.all_to_all(jnp.stack(jnp.split(acts_copies, lax.axis_size(('dp', 'exp...  4.74 us
    all_to_all x1, starting transfers between devices, shards(): lax.all_to_all(grad_copies, ('dp', 'expert'), split_axis=0, concat_axis=1...  4.1 us
    all_to_all x1, starting transfers between devices, shards(): lax.all_to_all(partial_value, ('dp', 'expert'), split_axis=1, concat_axis...  3.68 us
  transfers between devices with their start and end apart: 5, of which 4 were waited for; matrix products, arithmetic and copies ran while one was open for 33% of the time, Pallas kernels for 0%

profile of v1, /device:TPU:0, one launch (start us, length us, event | category | flops | bytes accessed | tf_op | source)
XLA Modules:
  0.0 84.2 jit_solution(5291984473666100653)
XLA Ops:
  0.6 0.9 %copy.28 = s32[1,128,6]{2,1,0:T(8,128)S(1)} copy(s32[1,128,6]{1,0,2:T(1,128)} %param.9) | data formatting | bytes 6144 | tf_op args[2]
  3.7 2.0 %gather_fusion.2 = bf16[16,3072]{1,0:T(8,128)(2,1)S(1)} fusion(bf16[128,3072]{1,0:T(8,128)(2,1)} %bitcast.149, s32[1024]{0:T(1024)S(1)} %get-tuple-element.53), kind=kCustom, calls=%fused_computation.2 | custom fusion | bytes 196672 | tf_op jit(solution)/shard_map/gather | solution.py:45
  10.8 5.2 %all-to-all-start.1 = ((bf16[8,1,8,3072]{3,2,1,0:T(8,128)(2,1)}), bf16[8,1,8,3072]{3,2,1,0:T(8,128)(2,1)S(1)}, u32[]{:S(2)}, u32[]{:S(2)}) async-start(bf16[8,1,8,3072]{3,2,1,0:T(8,128)(2,1)} %fusion.23), calls=%async_computation.1 | async-start | bytes 786432 | tf_op jit(solution)/shard_map/all_to_all | solution.py:58
  18.7 4.7 %all-to-all-done.1 = bf16[8,1,8,3072]{3,2,1,0:T(8,128)(2,1)S(1)} async-done(((bf16[8,1,8,3072]{3,2,1,0:T(8,128)(2,1)}), bf16[8,1,8,3072]{3,2,1,0:T(8,128)(2,1)S(1)}, u32[]{:S(2)}, u32[]{:S(2)}) %all-to-all-start.1) | async-done | bytes 393248 | tf_op jit(solution)/shard_map/all_to_all | solution.py:58
  23.4 1.7 %broadcast_in_dim.84 = bf16[4,2,8,3072]{3,2,1,0:T(8,128)(2,1)} broadcast(bf16[2,8,3072]{2,1,0:T(8,128)(2,1)} %fusion.20), dimensions={1,2,3} | broadcast | bytes 491520 | tf_op jit(solution)/shard_map/broadcast_in_dim | solution.py:53
  25.1 4.1 %all-to-all-start = ((bf16[8,8,3072]{2,1,0:T(8,128)(2,1)}), bf16[8,8,3072]{2,1,0:T(8,128)(2,1)}, u32[]{:S(2)}, u32[]{:S(2)}) async-start(bf16[8,8,3072]{2,1,0:T(8,128)(2,1)} %bitcast.148), calls=%async_computation | async-start | bytes 786432 | tf_op jit(solution)/shard_map/all_to_all | solution.py:66
  29.2 1.0 %fusion.6 = f32[64,256]{1,0:T(8,128)} fusion(bf16[1,1,3072,256]{3,2,1,0:T(8,128)(2,1)S(1)} %copy-done, bf16[8,1,8,3072]{3,2,1,0:T(8,128)(2,1)S(1)} %all-to-all-done.1), kind=kOutput, calls=%fused_computation.14 | convolution fusion | flops 100663296 | bytes 2031616 | tf_op jit(solution)/shard_map/erd,edh->erh/dot_general | solution.py:71
  30.2 1.0 %fusion.9 = f32[64,256]{1,0:T(8,128)} fusion(bf16[1,1,3072,256]{3,2,1,0:T(8,128)(2,1)S(1)} %copy-done.1, bf16[8,1,8,3072]{3,2,1,0:T(8,128)(2,1)S(1)} %all-to-all-done.1), kind=kOutput, calls=%fused_computation.17 | convolution fusion | flops 100663296 | bytes 2031616 | tf_op jit(solution)/shard_map/erd,edh->erh/dot_general | solution.py:72
  31.2 5.4 %all-to-all-done = bf16[8,8,3072]{2,1,0:T(8,128)(2,1)} async-done(((bf16[8,8,3072]{2,1,0:T(8,128)(2,1)}), bf16[8,8,3072]{2,1,0:T(8,128)(2,1)}, u32[]{:S(2)}, u32[]{:S(2)}) %all-to-all-start) | async-done | bytes 393248 | tf_op jit(solution)/shard_map/all_to_all | solution.py:66
  36.6 2.7 %multiply_reduce_fusion = (f32[64]{0:T(128)}, bf16[64,256]{1,0:T(8,128)(2,1)S(1)}, bf16[64,256]{1,0:T(8,128)(2,1)S(1)}) fusion(f32[64,256]{1,0:T(8,128)} %fusion.9, f32[64,256]{1,0:T(8,128)} %fusion.6, bf16[1,1,256,3072]{3,2,1,0:T(8,128)(2,1)} %param.13, bf16[8,8,3072]{2,1,0:T(8,128)(2,1)} %all-to-all-done), kind=kOutput, calls=%fused_computation.32 | convolution fusion | flops 100925376 | bytes 2162944 | tf_op jit(solution)/shard_map/erd,ehd->erh/dot_general | solution.py:75
  40.6 1.7 %copy.31 = f32[1,64,3072]{2,0,1:T(1,128)} copy(f32[1,64,3072]{2,1,0:T(8,128)S(1)} %fusion.3) | data formatting | bytes 1572864 | tf_op jit(solution)/shard_map/add | solution.py:95
  42.3 3.7 %all-to-all-start.2 = ((f32[1,64,3072]{2,0,1:T(1,128)}), f32[1,64,3072]{2,0,1:T(1,128)S(1)}, u32[]{:S(2)}, u32[]{:S(2)}) async-start(f32[1,64,3072]{2,0,1:T(1,128)} %copy.31), calls=%async_computation.2 | async-start | bytes 1572864 | tf_op jit(solution)/shard_map/all_to_all | solution.py:99
  47.5 1.7 %fusion.1 = bf16[1,1,3072,256]{3,2,1,0:T(8,128)(2,1)} fusion(bf16[64,256]{1,0:T(8,128)(2,1)S(1)} %copy-done.8, bf16[8,1,8,3072]{3,2,1,0:T(8,128)(2,1)S(1)} %all-to-all-done.1), kind=kOutput, calls=%fused_computation.7 | convolution fusion | flops 101449728 | bytes 1998848 | tf_op jit(solution)/shard_map/erd,erh->edh/dot_general | solution.py:92
  49.3 2.7 %fusion.2 = bf16[1,1,256,3072]{3,2,1,0:T(8,128)(2,1)} fusion(bf16[8,8,3072]{2,1,0:T(8,128)(2,1)} %all-to-all-done, f32[64,256]{1,0:T(8,128)S(1)} %copy-done.4, f32[64,256]{1,0:T(8,128)S(1)} %copy-done.3), kind=kOutput, calls=%fused_computation.8 | convolution fusion | flops 101548032 | bytes 2097152 | tf_op jit(solution)/shard_map/erh,erd->ehd/dot_general | solution.py:82
  52.0 5.6 %all-to-all-done.2 = f32[1,64,3072]{2,0,1:T(1,128)S(1)} async-done(((f32[1,64,3072]{2,0,1:T(1,128)}), f32[1,64,3072]{2,0,1:T(1,128)S(1)}, u32[]{:S(2)}, u32[]{:S(2)}) %all-to-all-start.2) | async-done | bytes 786464 | tf_op jit(solution)/shard_map/all_to_all | solution.py:99
  57.6 3.3 %all-to-all-start.3 = ((f32[1,8,8]{2,0,1:T(1,128)}), f32[1,8,8]{2,0,1:T(1,128)S(1)}, u32[]{:S(2)}, u32[]{:S(2)}) async-start(f32[1,8,8]{2,0,1:T(1,128)} %bitcast.25), calls=%async_computation.3 | async-start | bytes 8192 | tf_op jit(solution)/shard_map/all_to_all | solution.py:100
  61.1 1.2 %convolution_convert_fusion.3 = bf16[128,3072]{1,0:T(8,128)(2,1)S(1)} fusion(bf16[16,3072]{1,0:T(8,128)(2,1)S(1)} %reduce_sum.52, s32[16]{0:T(128)} %and_select_fusion.2, pred[16]{0:T(512)(128)(4,1)} %copy-done.11), kind=kOutput, calls=%fused_computation.9 | convolution fusion | flops 12980224 | bytes 884816 | tf_op jit(solution)/shard_map/st,sd->td/dot_general | solution.py:110
  62.2 3.7 %collective-permute-start = (bf16[128,3072]{1,0:T(8,128)(2,1)S(1)}, bf16[128,3072]{1,0:T(8,128)(2,1)S(1)}, u32[]{:S(2)}, u32[]{:S(2)}) collective-permute-start(bf16[128,3072]{1,0:T(8,128)(2,1)S(1)} %convolution_convert_fusion.3), channel_id=1, source_target_pairs={{0,24},{8,0},{16,8},{24,16},{1,25},{9,1},{17,9},{25,17},{2,26},{10... | collective-permute-start | bytes 2359304 | tf_op jit(solution)/shard_map/ppermute | solution.py:10
  65.9 2.5 %fusion = bf16[1,1,3072,256]{3,2,1,0:T(8,128)(2,1)} fusion(bf16[64,256]{1,0:T(8,128)(2,1)} %copy-done.6, bf16[8,1,8,3072]{3,2,1,0:T(8,128)(2,1)S(1)} %all-to-all-done.1), kind=kOutput, calls=%fused_computation.6 | convolution fusion | flops 101449728 | bytes 1998848 | tf_op jit(solution)/shard_map/erd,erh->edh/dot_general | solution.py:89
  70.4 4.4 %fusion.42 = (f32[768]{0:T(1024)S(1)}, s32[768,1]{0,1:T(1,128)S(1)}) fusion(f32[]{:T(128)} %bitcast.35, f32[]{:T(128)} %bitcast.36, f32[]{:T(128)} %bitcast.37, f32[]{:T(128)} %bitcast.38, f32[]{:T(128)} %bitcast.39, f32[]{:T(128)} %bitcast.41, f32[]{:T(128)} %bitcast.40, s32[768,1]{0,1:T(1,128)S(1)} %mul.82, pred[768,1]{0,1:T(4,128)(4,1)S(1)} %lt.81, ...), kind=kLoop, calls=%fused_computation.92 | loop fusion | flops 14592 | bytes 13084 | tf_op jit(solution)/shard_map/gather | solution.py:114
  74.9 5.6 %select_select_fusion = f32[768]{0:T(1024)S(1)} fusion(pred[768]{0:T(1024)(128)(4,1)S(1)} %get-tuple-element.29, pred[768]{0:T(1024)(128)(4,1)S(1)} %get-tuple-element.28, pred[768]{0:T(1024)(128)(4,1)S(1)} %get-tuple-element.27, pred[768]{0:T(1024)(128)(4,1)S(1)} %get-tuple-element.26, pred[768]{0:T(1024)(128)(4,1)S(1)} %get-tuple-element.25, ...), kind=kLoop, calls=%fused_computation.88 | loop fusion | flops 7680 | bytes 13860 | tf_op jit(solution)/shard_map/gather | solution.py:114
  80.7 0.9 %div.29 = f32[1,128,6]{2,1,0:T(8,128)S(1)} divide(f32[1,128,6]{2,1,0:T(8,128)S(1)} %gather.21, f32[1,128,6]{2,1,0:T(8,128)} %copy-done.5) | non-fusion elementwise | flops 768 | bytes 9216 | tf_op jit(solution)/shard_map/div | solution.py:114
  82.2 1.0 %collective-permute-done = bf16[128,3072]{1,0:T(8,128)(2,1)S(1)} collective-permute-done((bf16[128,3072]{1,0:T(8,128)(2,1)S(1)}, bf16[128,3072]{1,0:T(8,128)(2,1)S(1)}, u32[]{:S(2)}, u32[]{:S(2)}) %collective-permute-start) | collective-permute-done | bytes 786464 | tf_op jit(solution)/shard_map/ppermute | solution.py:10
  83.3 0.9 %copy.48 = bf16[1,128,3072]{2,1,0:T(8,128)(2,1)} copy(bf16[1,128,3072]{2,1,0:T(8,128)(2,1)S(1)} %bitcast.151) | data formatting | bytes 1572864
  (81 shorter events, 15.7 us)
Async XLA Ops:
  0.6 28.6 %copy-start = (bf16[1,1,3072,256]{3,2,1,0:T(8,128)(2,1)S(1)}, bf16[1,1,3072,256]{3,2,1,0:T(8,128)(2,1)}, u32[]{:S(2)}) copy-start(bf16[1,1,3072,256]{3,2,1,0:T(8,128)(2,1)} %param.11) | copy-start | bytes 4718596
  3.1 0.5 copy-start.11
  3.2 0.5 copy-start.13
  3.7 12.3 %copy-start.9 = (s32[1,128,6]{1,0,2:T(1,128)S(1)}, s32[1,128,6]{1,0,2:T(1,128)}, u32[]{:S(2)}) copy-start(s32[1,128,6]{1,0,2:T(1,128)} %param.9) | copy-start | bytes 9220
  3.7 12.6 %copy-start.10 = (f32[1,128,6]{1,0,2:T(1,128)S(1)}, f32[1,128,6]{1,0,2:T(1,128)}, u32[]{:S(2)}) copy-start(f32[1,128,6]{1,0,2:T(1,128)} %param.10) | copy-start | bytes 9220
  5.7 11.6 %copy-start.2 = (bf16[1,128,3072]{2,1,0:T(8,128)(2,1)S(1)}, bf16[1,128,3072]{2,1,0:T(8,128)(2,1)}, u32[]{:S(2)}) copy-start(bf16[1,128,3072]{2,1,0:T(8,128)(2,1)} %param.8) | copy-start | bytes 2359300
  10.8 12.6 %all-to-all-start.1 = ((bf16[8,1,8,3072]{3,2,1,0:T(8,128)(2,1)}), bf16[8,1,8,3072]{3,2,1,0:T(8,128)(2,1)S(1)}, u32[]{:S(2)}, u32[]{:S(2)}) async-start(bf16[8,1,8,3072]{3,2,1,0:T(8,128)(2,1)} %fusion.23), calls=%async_computation.1 | async-start | bytes 786432 | tf_op jit(solution)/shard_map/all_to_all | solution.py:58
  16.5 1.5 %copy-start.5 = (f32[1,128,6]{2,1,0:T(8,128)}, f32[1,128,6]{2,1,0:T(8,128)S(1)}, u32[]{:S(2)}) copy-start(f32[1,128,6]{2,1,0:T(8,128)S(1)} %copy.30) | copy-start | bytes 9220
  18.7 11.5 %copy-start.1 = (bf16[1,1,3072,256]{3,2,1,0:T(8,128)(2,1)S(1)}, bf16[1,1,3072,256]{3,2,1,0:T(8,128)(2,1)}, u32[]{:S(2)}) copy-start(bf16[1,1,3072,256]{3,2,1,0:T(8,128)(2,1)} %param.12) | copy-start | bytes 4718596
  25.1 11.5 %all-to-all-start = ((bf16[8,8,3072]{2,1,0:T(8,128)(2,1)}), bf16[8,8,3072]{2,1,0:T(8,128)(2,1)}, u32[]{:S(2)}, u32[]{:S(2)}) async-start(bf16[8,8,3072]{2,1,0:T(8,128)(2,1)} %bitcast.148), calls=%async_computation | async-start | bytes 786432 | tf_op jit(solution)/shard_map/all_to_all | solution.py:66
  39.3 0.6 copy-start.6
  39.3 0.6 copy-start.7
  40.5 5.7 %copy-start.14 = (s32[16]{0:T(128)S(1)}, s32[16]{0:T(128)}, u32[]{:S(2)}) copy-start(s32[16]{0:T(128)} %copy-done.13) | copy-start | bytes 196
  40.6 6.3 %copy-start.12 = (f32[64]{0:T(128)S(1)}, f32[64]{0:T(128)}, u32[]{:S(2)}) copy-start(f32[64]{0:T(128)} %get-tuple-element.32) | copy-start | bytes 772
  40.6 7.0 %copy-start.8 = (bf16[64,256]{1,0:T(8,128)(2,1)S(1)}, bf16[64,256]{1,0:T(8,128)(2,1)}, u32[]{:S(2)}) copy-start(bf16[64,256]{1,0:T(8,128)(2,1)} %copy-done.7) | copy-start | bytes 98308
  42.3 7.0 %copy-start.3 = (f32[64,256]{1,0:T(8,128)S(1)}, f32[64,256]{1,0:T(8,128)}, u32[]{:S(2)}) copy-start(f32[64,256]{1,0:T(8,128)} %fusion.6) | copy-start | bytes 196612
  42.3 7.0 %copy-start.4 = (f32[64,256]{1,0:T(8,128)S(1)}, f32[64,256]{1,0:T(8,128)}, u32[]{:S(2)}) copy-start(f32[64,256]{1,0:T(8,128)} %fusion.9) | copy-start | bytes 196612
  42.3 15.3 %all-to-all-start.2 = ((f32[1,64,3072]{2,0,1:T(1,128)}), f32[1,64,3072]{2,0,1:T(1,128)S(1)}, u32[]{:S(2)}, u32[]{:S(2)}) async-start(f32[1,64,3072]{2,0,1:T(1,128)} %copy.31), calls=%async_computation.2 | async-start | bytes 1572864 | tf_op jit(solution)/shard_map/all_to_all | solution.py:99
  57.6 10.8 %all-to-all-start.3 = ((f32[1,8,8]{2,0,1:T(1,128)}), f32[1,8,8]{2,0,1:T(1,128)S(1)}, u32[]{:S(2)}, u32[]{:S(2)}) async-start(f32[1,8,8]{2,0,1:T(1,128)} %bitcast.25), calls=%async_computation.3 | async-start | bytes 8192 | tf_op jit(solution)/shard_map/all_to_all | solution.py:100
  62.2 21.0 %collective-permute-start = (bf16[128,3072]{1,0:T(8,128)(2,1)S(1)}, bf16[128,3072]{1,0:T(8,128)(2,1)S(1)}, u32[]{:S(2)}, u32[]{:S(2)}) collective-permute-start(bf16[128,3072]{1,0:T(8,128)(2,1)S(1)} %convolution_convert_fusion.3), channel_id=1, source_target_pairs={{0,24},{8,0},{16,8},{24,16},{1,25},{9,1},{17,9},{25,17},{2,26},{10... | collective-permute-start | bytes 2359304 | tf_op jit(solution)/shard_map/ppermute | solution.py:10
